TPU v7x, 32 devices: a whole 2x2x4 slice. The times are simulated.
32 devices in a mesh: dp: 4 (over y, core), seq: 8 (over z, x).
Axes of the slice: x: 2, y: 2, z: 4, core: 2. Of those that a mesh axis runs over, the one named last changes fastest.
Arguments:
- layer_input: bfloat16 [4096, 8192], P(('dp', 'seq')), may hold values from -6 to 6
- queries: bfloat16 [4096, 4096], P(('dp', 'seq')), may hold values from -110 to 110, as said below
- key_states: bfloat16 [4096, 512], P(('dp', 'seq')), may hold values from -12 to 12, as said below
- value_states: bfloat16 [4096, 512], P(('dp', 'seq')), may hold values from -6 to 6
- out_grad: bfloat16 [4096, 4096], P(('dp', 'seq')), may hold values from -6 to 6
Outputs:
- query_grad: bfloat16 [4096, 4096], P(('dp', 'seq'))
- key_grad: bfloat16 [4096, 512], P(('dp', 'seq'))
- value_grad: bfloat16 [4096, 512], P(('dp', 'seq'))
- weight_grad: float32 [8192, 1024], P(('dp', 'seq'))
Inputs may be any that keep to these rules, and one draw needn't show every extreme that they name: `queries`: rows of rough scales; some queries may nearly coincide in direction with keys of earlier positions. `key_states`: rows of rough scales.
All inputs are finite; a program needn't handle non-finite values.
Results may differ from a plain program's by a relative error of at most 0.0051.
Values may be sent and summed in bfloat16 or wider, within the bound.
No kernel may reach another device: no remote copies, remote signals or barrier semaphores. Data moves between devices by JAX's collectives and lax.ppermute only.
A program may use at most 128 MiB of HBM per device.

v0:
```python
import math
import jax
import jax.numpy as jnp
from jax import lax
from jax.sharding import PartitionSpec as P

D = 8192
QH = 32
KVH = 4
HD = 128
NEGATIVE = -1e30


def local(layer_input, queries, key_states, value_states, out_grad):
    local_rows = layer_input.shape[0]
    cycle_size = lax.axis_size("seq")
    replicas = lax.axis_size("dp")
    position = lax.axis_index("seq")
    length = local_rows * cycle_size
    group = QH // KVH
    channels = KVH * HD
    scale = 1.0 / math.sqrt(HD)
    block = math.gcd(length, 512)
    key_all, value_all = (
        lax.all_gather(key_states, "seq", axis=0, tiled=True),
        lax.all_gather(value_states, "seq", axis=0, tiled=True),
    )
    query_heads = queries.reshape(local_rows, KVH, group, HD)
    grad_heads = out_grad.reshape(local_rows, KVH, group, HD)
    query_place = position * local_rows + jnp.arange(local_rows, dtype=jnp.int32)
    needed = (position * local_rows + local_rows + block - 1) // block

    def block_scores(begin):
        key_block = lax.dynamic_slice_in_dim(key_all, begin, block, 0).reshape(block, KVH, HD)
        value_block = lax.dynamic_slice_in_dim(value_all, begin, block, 0).reshape(block, KVH, HD)
        scores = (
            jnp.einsum("tkgd,skd->kgts", query_heads, key_block, preferred_element_type=jnp.float32)
            * scale
        )
        key_place = begin + jnp.arange(block, dtype=jnp.int32)
        visible = key_place[None, :] <= query_place[:, None]
        scores = jnp.where(visible, scores, NEGATIVE)
        grad_probs = jnp.einsum(
            "tkgd,skd->kgts", grad_heads, value_block, preferred_element_type=jnp.float32
        )
        return (key_block, scores, grad_probs)

    def first_pass(step_index, carry):
        row_max, denom, weighted = carry
        key_block, scores, grad_probs = block_scores(step_index * block)
        new_max = jnp.maximum(row_max, jnp.max(scores, axis=-1))
        factor = jnp.exp(row_max - new_max)
        expon = jnp.exp(scores - new_max[..., None])
        return (
            new_max,
            denom * factor + jnp.sum(expon, axis=-1),
            weighted * factor + jnp.sum(expon * grad_probs, axis=-1),
        )

    stats_shape = (KVH, group, local_rows)
    start_stats = (
        jnp.full(stats_shape, NEGATIVE, jnp.float32),
        jnp.zeros(stats_shape, jnp.float32),
        jnp.zeros(stats_shape, jnp.float32),
    )
    row_max, denom, weighted = lax.fori_loop(0, needed, first_pass, start_stats)
    delta = weighted / denom

    def second_pass(step_index, carry):
        grad_query, terms = carry
        begin = step_index * block
        key_block, scores, grad_probs = block_scores(begin)
        probs = jnp.exp(scores - row_max[..., None]) / denom[..., None]
        grad_scores = (scale * probs * (grad_probs - delta[..., None])).astype(jnp.bfloat16)
        probs_low = probs.astype(jnp.bfloat16)
        grad_query = grad_query + jnp.einsum(
            "kgts,skd->tkgd", grad_scores, key_block, preferred_element_type=jnp.float32
        )
        key_part = jnp.einsum(
            "kgts,tkgd->skd", grad_scores, query_heads, preferred_element_type=jnp.float32
        )
        value_part = jnp.einsum(
            "kgts,tkgd->skd", probs_low, grad_heads, preferred_element_type=jnp.float32
        )
        joined = jnp.concatenate(
            [key_part.reshape(block, channels), value_part.reshape(block, channels)], axis=1
        )
        terms = lax.dynamic_update_slice_in_dim(terms, joined, begin, 0)
        return (grad_query, terms)

    start_grads = (
        jnp.zeros((local_rows, KVH, group, HD), jnp.float32),
        jnp.zeros((length, 2 * channels), jnp.float32),
    )
    grad_query, terms = lax.fori_loop(0, needed, second_pass, start_grads)
    query_grad = grad_query.reshape(local_rows, QH * HD).astype(jnp.bfloat16)
    owned_grads = lax.psum_scatter(terms, "seq", scatter_dimension=0, tiled=True).astype(
        jnp.bfloat16
    )
    summed_grads = lax.all_gather(owned_grads, "seq", axis=0, tiled=True)
    slab = D // (replicas * cycle_size)
    columns = lax.all_to_all(
        layer_input.reshape(local_rows, replicas, cycle_size, slab),
        "seq",
        split_axis=2,
        concat_axis=0,
        tiled=True,
    )
    columns = columns.reshape(length, replicas * slab)
    weight_grad = lax.psum_scatter(
        jnp.einsum("tr,tc->rc", columns, summed_grads, preferred_element_type=jnp.float32),
        "dp",
        scatter_dimension=0,
        tiled=True,
    )
    return (query_grad, owned_grads[:, :channels], owned_grads[:, channels:], weight_grad)


def solution(mesh):
    in_specs = (
        P(("dp", "seq"), None),
        P(("dp", "seq"), None),
        P(("dp", "seq"), None),
        P(("dp", "seq"), None),
        P(("dp", "seq"), None),
    )
    out_specs = (
        P(("dp", "seq"), None),
        P(("dp", "seq"), None),
        P(("dp", "seq"), None),
        P(("dp", "seq"), None),
    )
    return jax.shard_map(local, mesh=mesh, in_specs=in_specs, out_specs=out_specs, check_vma=False)
```

profile of v0, /device:TPU:0, one launch (start us, length us, event | category | flops | bytes accessed | tf_op | source)
XLA Modules:
  0.0 388.9 jit_solution(6068416372018879133)
XLA Ops:
  7.2 0.0 all-gather.4.cloned.1.call-start
  7.2 1.7 copy.69
  8.9 0.0 all-gather.6.cloned.1.call-start
  8.9 1.7 copy.71
  10.6 0.0 reduce-scatter.3.cloned.1.call-start
  10.7 1.6 copy.70
  12.3 0.7 copy.73
  13.0 1.6 copy.72
  14.6 1.3 copy.74
  15.9 37.0 %all-gather.4.cloned.1.call-done = bf16[1024,512]{0,1:T(8,128)(2,1)} async-done(((bf16[128,512]{0,1:T(8,128)(2,1)}), bf16[1024,512]{0,1:T(8,128)(2,1)}) %all-gather.4.cloned.1.call-update) | async-done | bytes 1048592 | tf_op jit(solution)/shard_map/all_gather | solution.py:25
  52.9 41.1 %all-gather.6.cloned.1.call-done = bf16[1024,512]{0,1:T(8,128)(2,1)} async-done(((bf16[128,512]{0,1:T(8,128)(2,1)}), bf16[1024,512]{0,1:T(8,128)(2,1)}) %all-gather.6.cloned.1.call-update) | async-done | bytes 1048592 | tf_op jit(solution)/shard_map/all_gather | solution.py:26
  94.0 7.5 %while.28 = (s32[]{:T(128)}, f32[4,8,128]{2,1,0:T(8,128)S(1)}, f32[4,8,128]{2,1,0:T(8,128)S(1)}, f32[4,8,128]{2,1,0:T(8,128)S(1)}, s32[]{:T(128)}, /*index=5*/bf...) while((s32[]{:T(128)}, f32[4,8,128]{2,1,0:T(8,128)S(1)}, ...), condition=%wide.region_4.5_spmd.clone, body=%wide.region_0.4_spmd.clone.sunk | while | flops 1098986112 | bytes 35165400 | solution.py:66
  94.0 1.3 constant_dynamic-slice_fusion.6
  95.3 0.1 broadcast_compare_fusion.4
  95.4 1.5 fusion.57
  96.9 1.8 fusion.59
  98.7 2.7 fusion.58
  101.5 2.5 broadcast_in_dim.32.clone
  104.0 1.6 broadcast_in_dim.31
  105.6 19.8 %while.29 = (s32[]{:T(128)}, f32[128,4,8,128]{0,3,2,1:T(8,128)}, f32[1024,1024]{1,0:T(8,128)}, s32[]{:T(128)}, bf16[1024,512]{0,1:T(8,128)(2,1)}, /*index=5*/bf1...) while((s32[]{:T(128)}, f32[128,4,8,128]{0,3,2,1:T(8,128)}, ...), condition=%wide.region_6.7_spmd.clone, body=%wide.region_5.6_spmd.clone.sunk | while | flops 2704343552 | bytes 108713312 | solution.py:95
  105.6 1.6 constant_dynamic-slice_fusion.7
  107.3 0.1 broadcast_compare_fusion.5
  107.4 2.3 fusion.70
  109.8 1.7 fusion.71
  111.5 1.5 fusion.73
  113.0 0.5 copy-done
  113.4 1.5 fusion.72
  114.9 1.5 pad_maximum_fusion.2
  116.4 1.9 copy.110
  118.4 1.5 constant_dynamic-update-slice_fusion.2
  119.8 1.5 copy-done.1
  121.3 4.1 %bitcast_add_fusion.2 = f32[128,4,8,128]{0,3,2,1:T(8,128)} fusion(f32[128,4,8,128]{0,3,2,1:T(8,128)} %get-tuple-element.501, bf16[512,4,128,1]{0,2,3,1:T(8,128)(2,1)} %bitcast.153, bf16[4,8,128,512]{2,3,1,0:T(8,128)(2,1)S(1)} %copy-done.1), kind=kOutput, calls=%fused_computation.26.clone.1 | convolution fusion | flops 537395200 | bytes 8912896 | tf_op jit(solution)/shard_map/while/body/kgts,skd->tkgd/dot_general | solution.py:76
  125.4 3.2 copy.77
  128.6 1.5 copy.78
  130.1 30.8 %all-to-all-start = ((bf16[128,4,8,256]{0,3,1,2:T(8,128)(2,1)}), bf16[128,4,8,256]{0,3,1,2:T(8,128)(2,1)S(1)}, u32[]{:S(2)}, u32[]{:S(2)}) async-start(bf16[128,4,8,256]{0,3,1,2:T(8,128)(2,1)} %copy.78), calls=%async_computation.1 | async-start | bytes 4194304 | tf_op jit(solution)/shard_map/all_to_all | solution.py:102
  160.9 0.0 all-gather.8.cloned.1.call-start
  161.0 117.2 %reduce-scatter.3.cloned.1.call-done = f32[128,1024]{1,0:T(8,128)} async-done(((f32[1024,1024]{1,0:T(8,128)}), f32[128,1024]{1,0:T(8,128)}) %reduce-scatter.3.cloned.1.call-update) | async-done | bytes 524304 | tf_op jit(solution)/shard_map/reduce_scatter | solution.py:97
  278.2 1.8 convert_element_type.17
  280.0 0.3 reduce-scatter.5.cloned.1.call-start
  280.3 2.7 copy.79
  283.0 47.1 %all-gather.8.cloned.1.call-done = bf16[1024,1024]{1,0:T(8,128)(2,1)} async-done(((bf16[128,1024]{1,0:T(8,128)(2,1)}), bf16[1024,1024]{1,0:T(8,128)(2,1)}) %all-gather.8.cloned.1.call-update) | async-done | bytes 2097168 | tf_op jit(solution)/shard_map/all_gather | solution.py:100
  330.0 6.6 %convolution_bitcast_fusion = f32[1024,1024]{0,1:T(8,128)} fusion(bf16[1024,1024]{1,0:T(8,128)(2,1)} %all-gather.8.cloned.1.call-done, bf16[128,8,8,128]{3,2,1,0:T(8,128)(2,1)} %bitcast.159), kind=kOutput, calls=%fused_computation.33 | convolution fusion | flops 2147483648 | bytes 8388608 | tf_op jit(solution)/shard_map/tr,tc->rc/dot_general | solution.py:111
  336.6 1.6 copy-done.2
  338.2 0.2 convert_element_type.15
  338.4 1.3 copy.93
  339.7 0.7 fusion.16
  340.4 39.4 %reduce-scatter.5.cloned.1.call-done = f32[256,1024]{0,1:T(8,128)} async-done(((f32[1024,1024]{0,1:T(8,128)}), f32[256,1024]{0,1:T(8,128)}) %reduce-scatter.5.cloned.1.call-update) | async-done | bytes 1048592 | tf_op jit(solution)/shard_map/reduce_scatter | solution.py:110
  379.8 2.5 copy.80
  (30 shorter events, 0.2 us)
Async XLA Ops:
  7.2 45.7 %all-gather.4.cloned.1.call-start = ((), (), s32[]{:S(2)}) async-start(), calls=%async_computation.3 | async-start | bytes 1179648 | tf_op jit(solution)/shard_map/all_gather | solution.py:25
  8.9 85.1 %all-gather.6.cloned.1.call-start = ((), (), s32[]{:S(2)}) async-start(), calls=%async_computation.4 | async-start | bytes 1179648 | tf_op jit(solution)/shard_map/all_gather | solution.py:26
  10.6 267.5 %reduce-scatter.3.cloned.1.call-start = ((), (), s32[]{:S(2)}) async-start(), calls=%async_computation.5 | async-start | bytes 4718592 | tf_op jit(solution)/shard_map/reduce_scatter | solution.py:97
  96.9 1.8 copy-start.7
  105.6 5.8 %copy-start.3 = (bf16[128,4,8,128]{0,3,2,1:T(8,128)(2,1)}, bf16[128,4,8,128]{0,3,2,1:T(8,128)(2,1)S(1)}, u32[]{:S(2)}) copy-start(bf16[128,4,8,128]{0,3,2,1:T(8,128)(2,1)S(1)} %get-tuple-element.521) | copy-start | bytes 3145732 | tf_op jit(solution)/shard_map/while
  107.2 2.5 copy-start.5
  111.5 2.0 copy-start
  118.3 2.9 copy-start.1
  121.3 4.1 %copy-start.4 = (bf16[128,4,8,128]{0,3,2,1:T(8,128)(2,1)S(1)}, bf16[128,4,8,128]{0,3,2,1:T(8,128)(2,1)}, u32[]{:S(2)}) copy-start(bf16[128,4,8,128]{0,3,2,1:T(8,128)(2,1)} %copy-done.3) | copy-start | bytes 3145732 | tf_op jit(solution)/shard_map/while
  130.1 150.1 %all-to-all-start = ((bf16[128,4,8,256]{0,3,1,2:T(8,128)(2,1)}), bf16[128,4,8,256]{0,3,1,2:T(8,128)(2,1)S(1)}, u32[]{:S(2)}, u32[]{:S(2)}) async-start(bf16[128,4,8,256]{0,3,1,2:T(8,128)(2,1)} %copy.78), calls=%async_computation.1 | async-start | bytes 4194304 | tf_op jit(solution)/shard_map/all_to_all | solution.py:102
  160.9 169.1 %all-gather.8.cloned.1.call-start = ((), (), s32[]{:S(2)}) async-start(), calls=%async_computation.6 | async-start | bytes 2359296 | tf_op jit(solution)/shard_map/all_gather | solution.py:100
  280.0 99.8 %reduce-scatter.5.cloned.1.call-start = ((), (), s32[]{:S(2)}) async-start(), calls=%async_computation.7 | async-start | bytes 5242880 | tf_op jit(solution)/shard_map/reduce_scatter | solution.py:110
  336.6 1.6 copy-start.2
  336.6 3.1 copy-start.6
Sparse Core Ops, SparseCore 0:
  10.6 42.2 all-gather.3
  55.5 38.4 all-gather.5
  125.5 152.5 reduce-scatter.2
  280.9 49.0 all-gather.7
  336.8 42.9 reduce-scatter.4
where the time goes:
time: 390 us; the launch traced here: 389 us
  waiting for transfers between devices  282 us (72%)
  local copies, waits for them, and re-layouts  34.5 us (9%)
  starting transfers between devices  31.2 us (8%)
  matrix products  21.8 us (6%)
  between operations  13.9 us (4%)
  other arithmetic  5.56 us (1%)
    reduce_scatter x1, waiting for transfers between devices, local(): lax.psum_scatter(terms, 'seq', scatter_dimension=0, tiled=True)  117 us
    all_gather x1, waiting for transfers between devices, local(): summed_grads = lax.all_gather(owned_grads, 'seq', axis=0, tiled=True)  47.1 us
    all_gather x1, waiting for transfers between devices, local(): lax.all_gather(value_states, 'seq', axis=0, tiled=True)  41.1 us
    reduce_scatter x1, waiting for transfers between devices, local(): lax.psum_scatter(jnp.einsum('tr,tc->rc', columns, summed_grads, preferred...  39.4 us
    all_gather x1, waiting for transfers between devices, local(): lax.all_gather(key_states, 'seq', axis=0, tiled=True)  37 us
    all_to_all x1, starting transfers between devices, local(): lax.all_to_all(layer_input.reshape(local_rows, replicas, cycle_size, slab...  30.8 us
    unnamed x12, local copies, waits for them, and re-layouts  15.9 us
  transfers between devices with their start and end apart: 6, of which 5 were waited for; matrix products, arithmetic and copies ran while one was open for 5% of the time, Pallas kernels for 0%

commit v1 on v0

--- a/solution.py
+++ b/solution.py
@@ -1,3 +1,4 @@
+import functools
 import math
 import jax
 import jax.numpy as jnp
@@ -11,6 +12,39 @@
 NEGATIVE = -1e30
 
 
+def panels_get(page, at_axis):
+    answer = list(page.shape[1:])
+    answer[at_axis] *= page.shape[0]
+    return jnp.moveaxis(page, 0, at_axis).reshape(answer)
+
+
+def clear_masks_by_axis(work_x, mesh_dim, dim_no):
+    axis_total = lax.axis_size(mesh_dim)
+    leaves = [(dev, (dev + 1) % axis_total) for dev in range(axis_total)]
+    e_next, plain = ([], [])
+    stack_in = [(b, hop_no) for hop_no, b in leaves]
+    for c in [*range(axis_total - 1)]:
+        if c % 2 == 0:
+            side_arr = lax.ppermute(
+                e_next[-1] if e_next else work_x, axis_name=mesh_dim, perm=leaves
+            )
+            e_next.append(side_arr)
+        else:
+            far_arr = lax.ppermute(
+                plain[-1] if plain else work_x, perm=stack_in, axis_name=mesh_dim
+            )
+            plain.append(far_arr)
+    carry_out = jnp.stack([*e_next[::-1], work_x, *plain], axis=0)
+    work_now = len(e_next)
+    state_next = lax.axis_index(mesh_dim)
+    tile_out = state_next - work_now
+    carry_out = carry_out[(jnp.arange(axis_total) - tile_out) % axis_total]
+    return panels_get(carry_out, dim_no)
+
+
+_cover_edge = functools.partial(clear_masks_by_axis, mesh_dim="seq", dim_no=0)
+
+
 def local(layer_input, queries, key_states, value_states, out_grad):
     local_rows = layer_input.shape[0]
     cycle_size = lax.axis_size("seq")
@@ -22,7 +56,7 @@
     scale = 1.0 / math.sqrt(HD)
     block = math.gcd(length, 512)
     key_all, value_all = (
-        lax.all_gather(key_states, "seq", axis=0, tiled=True),
+        _cover_edge(key_states),
         lax.all_gather(value_states, "seq", axis=0, tiled=True),
     )
     query_heads = queries.reshape(local_rows, KVH, group, HD)

time: 390 us -> 364 us (0.933)
  waiting for transfers between devices: 282 us -> 227 us
  starting transfers between devices: 31.2 us -> 48.5 us
  local copies, waits for them, and re-layouts: 34.5 us -> 46.9 us
    all_gather x1 -> x0, waiting for transfers between devices: 37 us -> none  [local(): lax.all_gather(key_states, 'seq', axis=0, tiled=True)]
    all_gather x1, waiting for transfers between devices: 41.1 us -> 11.8 us  [local(): lax.all_gather(value_states, 'seq', axis=0, tiled=True)]
    ppermute x0 -> x7, starting transfers between devices: none -> 17.3 us  [the longest x3 14.2 us: clear_masks_by_axis(): lax.ppermute(plain[-1] if plain else work_x, perm=stack_in, axis_name=mes...]
    ppermute x0 -> x7, waiting for transfers between devices: none -> 11.1 us  [the longest x4 11.1 us: clear_masks_by_axis(): lax.ppermute(e_next[-1] if e_next else work_x, axis_name=mesh_dim, perm=l...]
    unnamed x12 -> x22, local copies, waits for them, and re-layouts: 15.9 us -> 22.5 us
  transfers between devices with their start and end apart: 6 -> 12, of which waited for: 5 -> 7; matrix products, arithmetic and copies ran while one was open for 5% -> 9% of each run, Pallas kernels for 0% -> 0%
where the time goes in v1:
time: 364 us
  waiting for transfers between devices  227 us (62%)
  starting transfers between devices  48.5 us (13%)
  local copies, waits for them, and re-layouts  46.9 us (13%)
  matrix products  21.8 us (6%)
  between operations  13.9 us (4%)
  other arithmetic  5.58 us (2%)
    reduce_scatter x1, waiting for transfers between devices, local(): lax.psum_scatter(terms, 'seq', scatter_dimension=0, tiled=True)  117 us
    all_gather x1, waiting for transfers between devices, local(): summed_grads = lax.all_gather(owned_grads, 'seq', axis=0, tiled=True)  47.2 us
    reduce_scatter x1, waiting for transfers between devices, local(): lax.psum_scatter(jnp.einsum('tr,tc->rc', columns, summed_grads, preferred...  39.4 us
    all_to_all x1, starting transfers between devices, local(): lax.all_to_all(layer_input.reshape(local_rows, replicas, cycle_size, slab...  30.8 us
    unnamed x22, local copies, waits for them, and re-layouts  22.5 us
    ppermute x3, starting transfers between devices, clear_masks_by_axis(): lax.ppermute(plain[-1] if plain else work_x, perm=stack_in, axis_name=mes...  14.2 us
    all_gather x1, waiting for transfers between devices, local(): lax.all_gather(value_states, 'seq', axis=0, tiled=True)  11.8 us
    ppermute x4, waiting for transfers between devices, clear_masks_by_axis(): lax.ppermute(e_next[-1] if e_next else work_x, axis_name=mesh_dim, perm=l...  11.1 us
  transfers between devices with their start and end apart: 12, of which 7 were waited for; matrix products, arithmetic and copies ran while one was open for 9% of the time, Pallas kernels for 0%

profile of v1, /device:TPU:0, one launch (start us, length us, event | category | flops | bytes accessed | tf_op | source)
XLA Modules:
  0.0 363.5 jit_solution(8708284127801936568)
XLA Ops:
  7.2 3.0 collective-permute-start
  10.2 6.7 %collective-permute-done = bf16[128,512]{1,0:T(8,128)(2,1)S(1)} collective-permute-done((bf16[128,512]{1,0:T(8,128)(2,1)}, bf16[128,512]{1,0:T(8,128)(2,1)S(1)}, u32[]{:S(2)}, u32[]{:S(2)}) %collective-permute-start) | collective-permute-done | bytes 131104 | tf_op jit(solution)/shard_map/ppermute | solution.py:28
  17.0 4.7 %collective-permute-start.4 = (bf16[128,512]{1,0:T(8,128)(2,1)}, bf16[128,512]{1,0:T(8,128)(2,1)S(1)}, u32[]{:S(2)}, u32[]{:S(2)}) collective-permute-start(bf16[128,512]{1,0:T(8,128)(2,1)} %param.11), channel_id=1, source_target_pairs={{1,0},{2,1},{3,2},{4,3},{5,4},{6,5},{7,6},{0,7},{9,8},{10,9},{11,1... | collective-permute-start | bytes 393224 | tf_op jit(solution)/shard_map/ppermute | solution.py:33
  21.7 3.0 collective-permute-done.1
  24.7 1.7 copy.71
  26.5 4.7 %collective-permute-start.5 = (bf16[128,512]{1,0:T(8,128)(2,1)S(1)}, bf16[128,512]{1,0:T(8,128)(2,1)}, u32[]{:S(2)}, u32[]{:S(2)}) collective-permute-start(bf16[128,512]{1,0:T(8,128)(2,1)S(1)} %collective-permute-done.4), channel_id=1, source_target_pairs={{1,0},{2,1},{3,2},{4,3},{5,4},{6,5},{7,6},{0,7},{9,8},{10,9},{11,1... | collective-permute-start | bytes 393224 | tf_op jit(solution)/shard_map/ppermute | solution.py:33
  31.2 1.3 collective-permute-done.2
  32.6 1.6 copy.70
  34.9 1.6 copy.72
  36.5 1.3 copy.74
  37.9 4.8 %collective-permute-start.6 = (bf16[128,512]{1,0:T(8,128)(2,1)}, bf16[128,512]{1,0:T(8,128)(2,1)S(1)}, u32[]{:S(2)}, u32[]{:S(2)}) collective-permute-start(bf16[128,512]{1,0:T(8,128)(2,1)} %collective-permute-done.5), channel_id=1, source_target_pairs={{1,0},{2,1},{3,2},{4,3},{5,4},{6,5},{7,6},{0,7},{9,8},{10,9},{11,1... | collective-permute-start | bytes 393224 | tf_op jit(solution)/shard_map/ppermute | solution.py:33
  42.6 1.6 bitcast_dynamic-update-slice_fusion.7
  44.2 1.6 bitcast_dynamic-update-slice_fusion.6
  45.8 1.6 bitcast_dynamic-update-slice_fusion.5
  49.3 1.6 bitcast_dynamic-update-slice_fusion.1
  51.6 2.8 gather_fusion
  54.4 2.3 copy.93
  56.6 11.8 %all-gather.3.cloned.1.call-done = bf16[1024,512]{0,1:T(8,128)(2,1)} async-done(((bf16[128,512]{0,1:T(8,128)(2,1)}), bf16[1024,512]{0,1:T(8,128)(2,1)}) %all-gather.3.cloned.1.call-update) | async-done | bytes 1048592 | tf_op jit(solution)/shard_map/all_gather | solution.py:60
  68.4 7.5 %while.28 = (s32[]{:T(128)}, f32[4,8,128]{2,1,0:T(8,128)S(1)}, f32[4,8,128]{2,1,0:T(8,128)S(1)}, f32[4,8,128]{2,1,0:T(8,128)S(1)}, s32[]{:T(128)}, /*index=5*/bf...) while((s32[]{:T(128)}, f32[4,8,128]{2,1,0:T(8,128)S(1)}, ...), condition=%wide.region_4.5_spmd.clone, body=%wide.region_0.4_spmd.clone.sunk | while | flops 1098986112 | bytes 35165400 | solution.py:100
  68.4 1.3 constant_dynamic-slice_fusion.6
  69.9 1.5 fusion.59
  71.4 1.8 fusion.61
  73.2 2.7 fusion.60
  76.0 2.5 broadcast_in_dim.33.clone
  78.4 1.6 broadcast_in_dim.32
  80.1 19.8 %while.29 = (s32[]{:T(128)}, f32[128,4,8,128]{0,3,2,1:T(8,128)}, f32[1024,1024]{1,0:T(8,128)}, s32[]{:T(128)}, bf16[1024,512]{0,1:T(8,128)(2,1)}, /*index=5*/bf1...) while((s32[]{:T(128)}, f32[128,4,8,128]{0,3,2,1:T(8,128)}, ...), condition=%wide.region_6.7_spmd.clone, body=%wide.region_5.6_spmd.clone.sunk | while | flops 2704343552 | bytes 108713312 | solution.py:129
  80.1 1.6 constant_dynamic-slice_fusion.7
  81.9 2.3 fusion.72
  84.2 1.7 fusion.73
  85.9 1.5 fusion.75
  87.9 1.5 fusion.74
  89.4 1.5 pad_maximum_fusion.2
  90.9 1.9 copy.111
  92.8 1.5 constant_dynamic-update-slice_fusion.2
  94.3 1.5 copy-done.1
  95.8 4.1 %bitcast_add_fusion.2 = f32[128,4,8,128]{0,3,2,1:T(8,128)} fusion(f32[128,4,8,128]{0,3,2,1:T(8,128)} %get-tuple-element.501, bf16[512,4,128,1]{0,2,3,1:T(8,128)(2,1)} %bitcast.172, bf16[4,8,128,512]{2,3,1,0:T(8,128)(2,1)S(1)} %copy-done.1), kind=kOutput, calls=%fused_computation.27.clone.1 | convolution fusion | flops 537395200 | bytes 8912896 | tf_op jit(solution)/shard_map/while/body/kgts,skd->tkgd/dot_general | solution.py:110
  99.9 3.2 copy.77
  103.2 1.5 copy.78
  104.7 30.8 %all-to-all-start = ((bf16[128,4,8,256]{0,3,1,2:T(8,128)(2,1)}), bf16[128,4,8,256]{0,3,1,2:T(8,128)(2,1)S(1)}, u32[]{:S(2)}, u32[]{:S(2)}) async-start(bf16[128,4,8,256]{0,3,1,2:T(8,128)(2,1)} %copy.78), calls=%async_computation.1 | async-start | bytes 4194304 | tf_op jit(solution)/shard_map/all_to_all | solution.py:136
  135.6 117.1 %reduce-scatter.3.cloned.1.call-done = f32[128,1024]{1,0:T(8,128)} async-done(((f32[1024,1024]{1,0:T(8,128)}), f32[128,1024]{1,0:T(8,128)}) %reduce-scatter.3.cloned.1.call-update) | async-done | bytes 524304 | tf_op jit(solution)/shard_map/reduce_scatter | solution.py:131
  252.7 1.8 convert_element_type.17
  254.8 2.7 copy.79
  257.5 47.2 %all-gather.5.cloned.1.call-done = bf16[1024,1024]{1,0:T(8,128)(2,1)} async-done(((bf16[128,1024]{1,0:T(8,128)(2,1)}), bf16[1024,1024]{1,0:T(8,128)(2,1)}) %all-gather.5.cloned.1.call-update) | async-done | bytes 2097168 | tf_op jit(solution)/shard_map/all_gather | solution.py:134
  304.7 6.5 %convolution_bitcast_fusion = f32[1024,1024]{0,1:T(8,128)} fusion(bf16[1024,1024]{1,0:T(8,128)(2,1)} %all-gather.5.cloned.1.call-done, bf16[128,8,8,128]{3,2,1,0:T(8,128)(2,1)} %bitcast.179), kind=kOutput, calls=%fused_computation.34 | convolution fusion | flops 2147483648 | bytes 8388608 | tf_op jit(solution)/shard_map/tr,tc->rc/dot_general | solution.py:145
  311.3 1.6 copy-done.2
  313.0 1.3 copy.94
  315.0 39.4 %reduce-scatter.5.cloned.1.call-done = f32[256,1024]{0,1:T(8,128)} async-done(((f32[1024,1024]{0,1:T(8,128)}), f32[256,1024]{0,1:T(8,128)}) %reduce-scatter.5.cloned.1.call-update) | async-done | bytes 1048592 | tf_op jit(solution)/shard_map/reduce_scatter | solution.py:144
  354.4 2.5 copy.80
  (56 shorter events, 5.6 us)
Async XLA Ops:
  7.2 61.3 %all-gather.3.cloned.1.call-start = ((), (), s32[]{:S(2)}) async-start(), calls=%async_computation.3 | async-start | bytes 1179648 | tf_op jit(solution)/shard_map/all_gather | solution.py:60
  7.2 9.7 %collective-permute-start = (bf16[128,512]{1,0:T(8,128)(2,1)}, bf16[128,512]{1,0:T(8,128)(2,1)S(1)}, u32[]{:S(2)}, u32[]{:S(2)}) collective-permute-start(bf16[128,512]{1,0:T(8,128)(2,1)} %param.11), channel_id=1, source_target_pairs={{0,1},{1,2},{2,3},{3,4},{4,5},{5,6},{6,7},{7,0},{8,9},{9,10},{10,1... | collective-permute-start | bytes 393224 | tf_op jit(solution)/shard_map/ppermute | solution.py:28
  16.9 7.7 %collective-permute-start.1 = (bf16[128,512]{1,0:T(8,128)(2,1)S(1)}, bf16[128,512]{1,0:T(8,128)(2,1)S(1)}, u32[]{:S(2)}, u32[]{:S(2)}) collective-permute-start(bf16[128,512]{1,0:T(8,128)(2,1)S(1)} %collective-permute-done), channel_id=1, source_target_pairs={{0,1},{1,2},{2,3},{3,4},{4,5},{5,6},{6,7},{7,0},{8,9},{9,10},{10,1... | collective-permute-start | bytes 393224 | tf_op jit(solution)/shard_map/ppermute | solution.py:28
  17.0 9.5 %collective-permute-start.4 = (bf16[128,512]{1,0:T(8,128)(2,1)}, bf16[128,512]{1,0:T(8,128)(2,1)S(1)}, u32[]{:S(2)}, u32[]{:S(2)}) collective-permute-start(bf16[128,512]{1,0:T(8,128)(2,1)} %param.11), channel_id=1, source_target_pairs={{1,0},{2,1},{3,2},{4,3},{5,4},{6,5},{7,6},{0,7},{9,8},{10,9},{11,1... | collective-permute-start | bytes 393224 | tf_op jit(solution)/shard_map/ppermute | solution.py:33
  24.7 9.5 %copy-start.9 = (bf16[128,512]{1,0:T(8,128)(2,1)}, bf16[128,512]{1,0:T(8,128)(2,1)S(1)}, u32[]{:S(2)}) copy-start(bf16[128,512]{1,0:T(8,128)(2,1)S(1)} %collective-permute-done.1) | copy-start | bytes 393220
  24.7 7.9 %collective-permute-start.2 = (bf16[128,512]{1,0:T(8,128)(2,1)S(1)}, bf16[128,512]{1,0:T(8,128)(2,1)}, u32[]{:S(2)}, u32[]{:S(2)}) collective-permute-start(bf16[128,512]{1,0:T(8,128)(2,1)S(1)} %collective-permute-done.1), channel_id=1, source_target_pairs={{0,1},{1,2},{2,3},{3,4},{4,5},{5,6},{6,7},{7,0},{8,9},{9,10},{10,1... | collective-permute-start | bytes 393224 | tf_op jit(solution)/shard_map/ppermute | solution.py:28
  26.4 226.3 %reduce-scatter.3.cloned.1.call-start = ((), (), s32[]{:S(2)}) async-start(), calls=%async_computation.4 | async-start | bytes 4718592 | tf_op jit(solution)/shard_map/reduce_scatter | solution.py:131
  26.5 11.4 %collective-permute-start.5 = (bf16[128,512]{1,0:T(8,128)(2,1)S(1)}, bf16[128,512]{1,0:T(8,128)(2,1)}, u32[]{:S(2)}, u32[]{:S(2)}) collective-permute-start(bf16[128,512]{1,0:T(8,128)(2,1)S(1)} %collective-permute-done.4), channel_id=1, source_target_pairs={{1,0},{2,1},{3,2},{4,3},{5,4},{6,5},{7,6},{0,7},{9,8},{10,9},{11,1... | collective-permute-start | bytes 393224 | tf_op jit(solution)/shard_map/ppermute | solution.py:33
  32.5 10.1 %collective-permute-start.3 = (bf16[128,512]{1,0:T(8,128)(2,1)}, bf16[128,512]{1,0:T(8,128)(2,1)}, u32[]{:S(2)}, u32[]{:S(2)}) collective-permute-start(bf16[128,512]{1,0:T(8,128)(2,1)} %collective-permute-done.2), channel_id=1, source_target_pairs={{0,1},{1,2},{2,3},{3,4},{4,5},{5,6},{6,7},{7,0},{8,9},{9,10},{10,1... | collective-permute-start | bytes 393224 | tf_op jit(solution)/shard_map/ppermute | solution.py:28
  34.2 13.8 %copy-start.8 = (bf16[128,512]{1,0:T(8,128)(2,1)S(1)}, bf16[128,512]{1,0:T(8,128)(2,1)}, u32[]{:S(2)}) copy-start(bf16[128,512]{1,0:T(8,128)(2,1)} %param.11) | copy-start | bytes 393220
  37.9 13.0 %collective-permute-start.6 = (bf16[128,512]{1,0:T(8,128)(2,1)}, bf16[128,512]{1,0:T(8,128)(2,1)S(1)}, u32[]{:S(2)}, u32[]{:S(2)}) collective-permute-start(bf16[128,512]{1,0:T(8,128)(2,1)} %collective-permute-done.5), channel_id=1, source_target_pairs={{1,0},{2,1},{3,2},{4,3},{5,4},{6,5},{7,6},{0,7},{9,8},{10,9},{11,1... | collective-permute-start | bytes 393224 | tf_op jit(solution)/shard_map/ppermute | solution.py:33
  71.4 1.8 copy-start.7
  80.1 5.8 %copy-start.3 = (bf16[128,4,8,128]{0,3,2,1:T(8,128)(2,1)}, bf16[128,4,8,128]{0,3,2,1:T(8,128)(2,1)S(1)}, u32[]{:S(2)}) copy-start(bf16[128,4,8,128]{0,3,2,1:T(8,128)(2,1)S(1)} %get-tuple-element.521) | copy-start | bytes 3145732 | tf_op jit(solution)/shard_map/while
  81.7 2.5 copy-start.5
  85.9 2.0 copy-start
  92.8 2.9 copy-start.1
  95.8 4.1 %copy-start.4 = (bf16[128,4,8,128]{0,3,2,1:T(8,128)(2,1)S(1)}, bf16[128,4,8,128]{0,3,2,1:T(8,128)(2,1)}, u32[]{:S(2)}) copy-start(bf16[128,4,8,128]{0,3,2,1:T(8,128)(2,1)} %copy-done.3) | copy-start | bytes 3145732 | tf_op jit(solution)/shard_map/while
  104.7 150.1 %all-to-all-start = ((bf16[128,4,8,256]{0,3,1,2:T(8,128)(2,1)}), bf16[128,4,8,256]{0,3,1,2:T(8,128)(2,1)S(1)}, u32[]{:S(2)}, u32[]{:S(2)}) async-start(bf16[128,4,8,256]{0,3,1,2:T(8,128)(2,1)} %copy.78), calls=%async_computation.1 | async-start | bytes 4194304 | tf_op jit(solution)/shard_map/all_to_all | solution.py:136
  135.5 169.2 %all-gather.5.cloned.1.call-start = ((), (), s32[]{:S(2)}) async-start(), calls=%async_computation.5 | async-start | bytes 2359296 | tf_op jit(solution)/shard_map/all_gather | solution.py:134
  254.5 99.9 %reduce-scatter.5.cloned.1.call-start = ((), (), s32[]{:S(2)}) async-start(), calls=%async_computation.6 | async-start | bytes 5242880 | tf_op jit(solution)/shard_map/reduce_scatter | solution.py:144
  311.3 1.6 copy-start.2
  311.3 3.1 copy-start.6
Sparse Core Ops, SparseCore 0:
  26.5 41.8 all-gather.2
  100.0 152.6 reduce-scatter.2
  255.6 49.0 all-gather.4
  311.4 42.9 reduce-scatter.4
